TPU v7x, 32 devices: a whole 2x2x4 slice. The times are simulated.
32 devices in a mesh: dp: 8 (over y, x, core), tensor: 4 (over z).
Axes of the slice: x: 2, y: 2, z: 4, core: 2. Of those that a mesh axis runs over, the one named last changes fastest.
Arguments:
- inputs: bfloat16 [16384, 768], P('dp'), may hold values from -6 to 6
- w_query: bfloat16 [768, 768], P(None, 'tensor'), may hold values from -0.21875 to 0.21875
- b_query: bfloat16 [768], P('tensor'), may hold values from -3 to 3
- w_key: bfloat16 [768, 768], P(None, 'tensor'), may hold values from -0.21875 to 0.21875
- w_value: bfloat16 [768, 768], P(None, 'tensor'), may hold values from -0.21875 to 0.21875
- b_value: bfloat16 [768], P('tensor'), may hold values from -3 to 3
- w_output: bfloat16 [768, 768], P('tensor'), may hold values from -6 to 6
- b_output: bfloat16 [768], replicated, may hold values from -3 to 3
- gain_attn: bfloat16 [768], replicated, may hold values from 0.5 to 1.5
- shift_attn: bfloat16 [768], replicated, may hold values from -3 to 3
- w_inner: bfloat16 [768, 3072], P(None, 'tensor'), may hold values from -0.21875 to 0.21875
- b_inner: bfloat16 [3072], P('tensor'), may hold values from -3 to 3
- w_outer: bfloat16 [3072, 768], P('tensor'), may hold values from -0.109375 to 0.109375
- b_outer: bfloat16 [768], replicated, may hold values from -3 to 3
- gain_ffn: bfloat16 [768], replicated, may hold values from 0.5 to 1.5
- shift_ffn: bfloat16 [768], replicated, may hold values from -3 to 3
- cotangent: bfloat16 [16384, 768], P('dp'), may hold values from -6 to 6
Outputs:
- layer_out: bfloat16 [16384, 768], P('dp')
- grad_inputs: float32 [16384, 768], P('dp')
- grad_w_query: float32 [768, 768], P('dp', 'tensor')
- grad_b_query: float32 [768], P('tensor')
- grad_w_key: float32 [768, 768], P('dp', 'tensor')
- grad_w_value: float32 [768, 768], P('dp', 'tensor')
- grad_b_value: float32 [768], P('tensor')
- grad_w_output: float32 [768, 768], P('tensor', 'dp')
- grad_b_output: float32 [768], replicated
- grad_gain_attn: float32 [768], replicated
- grad_shift_attn: float32 [768], replicated
- grad_w_inner: float32 [768, 3072], P('dp', 'tensor')
- grad_b_inner: float32 [3072], P('tensor')
- grad_w_outer: float32 [3072, 768], P('tensor', 'dp')
- grad_b_outer: float32 [768], replicated
- grad_gain_ffn: float32 [768], replicated
- grad_shift_ffn: float32 [768], replicated
All inputs are finite; a program needn't handle non-finite values.
Results may differ from a plain program's by a relative error of at most 0.014.
Values sent between devices are 32-bit elements; how exact they have to be, the bound alone decides.
No kernel may reach another device: no remote copies, remote signals or barrier semaphores. Data moves between devices by JAX's collectives and lax.ppermute only.
A program may use at most 128 MiB of HBM per device.

v0:
```python
from functools import partial
import jax
import jax.numpy as jnp
from jax import lax
from jax.sharding import PartitionSpec as P

HEAD_DIM = 64
LENGTH = 512
EPSILON = 1e-12


def norm_forward(values, gain, shift):
    center = values - jnp.mean(values, axis=-1, keepdims=True)
    inverse = lax.rsqrt(jnp.mean(center * center, axis=-1, keepdims=True) + EPSILON)
    normed = center * inverse
    return (normed * gain + shift, normed, inverse)


def norm_backward(upstream, gain, normed, inverse):
    scaled = upstream * gain
    first_mean = jnp.mean(scaled, axis=-1, keepdims=True)
    cross_mean = jnp.mean(scaled * normed, axis=-1, keepdims=True)
    grad_values = inverse * (scaled - first_mean - normed * cross_mean)
    return (grad_values, jnp.sum(upstream * normed, axis=0), jnp.sum(upstream, axis=0))


def contract_rows(left, right):
    return lax.dot_general(
        left, right, (((0,), (0,)), ((), ())), preferred_element_type=jnp.float32
    )


def times_transpose(left, right):
    return lax.dot_general(
        left, right, (((1,), (1,)), ((), ())), preferred_element_type=jnp.float32
    )


def column_sums(values):
    return jnp.sum(values.astype(jnp.float32), axis=0)


def attend_forward(query_seq, key_seq, value_seq, block_rows, scale):
    length, heads_here, head_size = query_seq.shape

    def one_block(query_block):
        scores = (
            jnp.einsum("qhd,khd->hqk", query_block, key_seq, preferred_element_type=jnp.float32)
            * scale
        )
        largest = jnp.max(scores, axis=-1, keepdims=True)
        expon = jnp.exp(scores - largest)
        totals = jnp.sum(expon, axis=-1, keepdims=True)
        probs = (expon / totals).astype(jnp.bfloat16)
        context = jnp.einsum("hqk,khd->qhd", probs, value_seq, preferred_element_type=jnp.float32)
        return (context.astype(jnp.bfloat16), largest[..., 0] + jnp.log(totals[..., 0]))

    blocks = query_seq.reshape(length // block_rows, block_rows, heads_here, head_size)
    context, log_totals = lax.map(one_block, blocks)
    return (context.reshape(length, heads_here * head_size), log_totals)


def attend_backward(query_seq, key_seq, value_seq, grad_context, log_totals, block_rows, scale):
    length, heads_here, head_size = query_seq.shape
    block_shape = (length // block_rows, block_rows, heads_here, head_size)

    def step(carry, pieces):
        grad_keys, grad_values = carry
        query_block, grad_block, lse_block = pieces
        scores = (
            jnp.einsum("qhd,khd->hqk", query_block, key_seq, preferred_element_type=jnp.float32)
            * scale
        )
        probs = jnp.exp(scores - lse_block[..., None])
        grad_values = grad_values + jnp.einsum(
            "hqk,qhd->khd",
            probs.astype(jnp.bfloat16),
            grad_block,
            preferred_element_type=jnp.float32,
        )
        grad_probs = jnp.einsum(
            "qhd,khd->hqk", grad_block, value_seq, preferred_element_type=jnp.float32
        )
        row_terms = jnp.sum(probs * grad_probs, axis=-1, keepdims=True)
        grad_scores = (probs * (grad_probs - row_terms)).astype(jnp.bfloat16)
        grad_query = (
            jnp.einsum("hqk,khd->qhd", grad_scores, key_seq, preferred_element_type=jnp.float32)
            * scale
        )
        grad_keys = (
            grad_keys
            + jnp.einsum(
                "hqk,qhd->khd", grad_scores, query_block, preferred_element_type=jnp.float32
            )
            * scale
        )
        return ((grad_keys, grad_values), grad_query.astype(jnp.bfloat16))

    zeros_init = jnp.zeros(key_seq.shape, jnp.float32)
    (grad_keys, grad_values), grad_query = lax.scan(
        step,
        (zeros_init, zeros_init),
        (query_seq.reshape(block_shape), grad_context.reshape(block_shape), log_totals),
    )
    flat = (length, heads_here * head_size)
    return (
        grad_query.reshape(flat),
        grad_keys.astype(jnp.bfloat16).reshape(flat),
        grad_values.astype(jnp.bfloat16).reshape(flat),
    )


def shards(
    inputs,
    w_query,
    b_query,
    w_key,
    w_value,
    b_value,
    w_output,
    b_output,
    gain_attn,
    shift_attn,
    w_inner,
    b_inner,
    w_outer,
    b_outer,
    gain_ffn,
    shift_ffn,
    cotangent,
):
    tok_rows = inputs.shape[0]
    heads_here = w_query.shape[1] // HEAD_DIM
    block_rows = min(512, LENGTH)
    scale = HEAD_DIM ** (-0.5)
    split_shape = (tok_rows // LENGTH, LENGTH, heads_here, HEAD_DIM)
    queries = (
        jnp.dot(inputs, w_query, preferred_element_type=jnp.float32) + b_query.astype(jnp.float32)
    ).astype(jnp.bfloat16)
    key_rows = jnp.dot(inputs, w_key, preferred_element_type=jnp.float32).astype(jnp.bfloat16)
    value_rows = (
        jnp.dot(inputs, w_value, preferred_element_type=jnp.float32) + b_value.astype(jnp.float32)
    ).astype(jnp.bfloat16)
    query_split = queries.reshape(split_shape)
    key_split = key_rows.reshape(split_shape)
    value_split = value_rows.reshape(split_shape)

    def forward_seq(triple):
        return attend_forward(triple[0], triple[1], triple[2], block_rows, scale)

    context, log_totals = lax.map(forward_seq, (query_split, key_split, value_split))
    context = context.reshape(tok_rows, heads_here * HEAD_DIM)
    attn_part = jnp.dot(context, w_output, preferred_element_type=jnp.float32)
    attn_total = lax.psum(attn_part, "tensor") + b_output.astype(jnp.float32)
    gain_one = gain_attn.astype(jnp.float32)
    gain_two = gain_ffn.astype(jnp.float32)
    hidden, normed_attn, inverse_attn = norm_forward(
        inputs.astype(jnp.float32) + attn_total, gain_one, shift_attn.astype(jnp.float32)
    )
    hidden_bf = hidden.astype(jnp.bfloat16)
    inner = jnp.dot(hidden_bf, w_inner, preferred_element_type=jnp.float32) + b_inner.astype(
        jnp.float32
    )
    active, gelu_pull = jax.vjp(partial(jax.nn.gelu, approximate=False), inner)
    active_bf = active.astype(jnp.bfloat16)
    outer_part = jnp.dot(active_bf, w_outer, preferred_element_type=jnp.float32)
    outer_total = lax.psum(outer_part, "tensor") + b_outer.astype(jnp.float32)
    layer_out, normed_ffn, inverse_ffn = norm_forward(
        hidden + outer_total, gain_two, shift_ffn.astype(jnp.float32)
    )
    grad_resid2, grad_gain_ffn, grad_shift_ffn = norm_backward(
        cotangent.astype(jnp.float32), gain_two, normed_ffn, inverse_ffn
    )
    grad_outer = grad_resid2.astype(jnp.bfloat16)
    grad_b_outer = column_sums(grad_outer)
    grad_w_outer = contract_rows(active_bf, grad_outer)
    grad_active = times_transpose(grad_outer, w_outer)
    grad_inner = gelu_pull(grad_active)[0].astype(jnp.bfloat16)
    grad_b_inner = column_sums(grad_inner)
    grad_w_inner = contract_rows(hidden_bf, grad_inner)
    grad_hidden = grad_resid2 + lax.psum(times_transpose(grad_inner, w_inner), "tensor")
    grad_resid1, grad_gain_attn, grad_shift_attn = norm_backward(
        grad_hidden, gain_one, normed_attn, inverse_attn
    )
    grad_attn = grad_resid1.astype(jnp.bfloat16)
    grad_b_output = column_sums(grad_attn)
    grad_w_output = contract_rows(context, grad_attn)
    grad_context = times_transpose(grad_attn, w_output).astype(jnp.bfloat16)

    def backward_seq(pieces):
        return attend_backward(
            pieces[0], pieces[1], pieces[2], pieces[3], pieces[4], block_rows, scale
        )

    grad_query, grad_key, grad_value = lax.map(
        backward_seq,
        (query_split, key_split, value_split, grad_context.reshape(split_shape), log_totals),
    )
    flat_shape = (tok_rows, heads_here * HEAD_DIM)
    grad_query = grad_query.reshape(flat_shape)
    grad_key = grad_key.reshape(flat_shape)
    grad_value = grad_value.reshape(flat_shape)
    grad_b_query = column_sums(grad_query)
    grad_b_value = column_sums(grad_value)
    grad_w_query = contract_rows(inputs, grad_query)
    grad_w_key = contract_rows(inputs, grad_key)
    grad_w_value = contract_rows(inputs, grad_value)
    input_part = (
        times_transpose(grad_query, w_query)
        + times_transpose(grad_key, w_key)
        + times_transpose(grad_value, w_value)
    )
    grad_inputs = grad_resid1 + lax.psum(input_part, "tensor")
    small_sums = lax.psum(
        (
            grad_b_query,
            grad_b_value,
            grad_b_output,
            grad_gain_attn,
            grad_shift_attn,
            grad_b_inner,
            grad_b_outer,
            grad_gain_ffn,
            grad_shift_ffn,
        ),
        "dp",
    )
    weight_shards = (
        lax.psum_scatter(grad_w_query, "dp", scatter_dimension=0, tiled=True),
        lax.psum_scatter(grad_w_key, "dp", scatter_dimension=0, tiled=True),
        lax.psum_scatter(grad_w_value, "dp", scatter_dimension=0, tiled=True),
        lax.psum_scatter(grad_w_output, "dp", scatter_dimension=1, tiled=True),
        lax.psum_scatter(grad_w_inner, "dp", scatter_dimension=0, tiled=True),
        lax.psum_scatter(grad_w_outer, "dp", scatter_dimension=1, tiled=True),
    )
    return (
        layer_out.astype(jnp.bfloat16),
        grad_inputs,
        weight_shards[0],
        small_sums[0],
        weight_shards[1],
        weight_shards[2],
        small_sums[1],
        weight_shards[3],
        small_sums[2],
        small_sums[3],
        small_sums[4],
        weight_shards[4],
        small_sums[5],
        weight_shards[5],
        small_sums[6],
        small_sums[7],
        small_sums[8],
    )


def solution(mesh):
    in_specs = (
        P("dp", None),
        P(None, "tensor"),
        P("tensor"),
        P(None, "tensor"),
        P(None, "tensor"),
        P("tensor"),
        P("tensor", None),
        P(),
        P(),
        P(),
        P(None, "tensor"),
        P("tensor"),
        P("tensor", None),
        P(),
        P(),
        P(),
        P("dp", None),
    )
    out_specs = (
        P("dp", None),
        P("dp", None),
        P("dp", "tensor"),
        P("tensor"),
        P("dp", "tensor"),
        P("dp", "tensor"),
        P("tensor"),
        P("tensor", "dp"),
        P(),
        P(),
        P(),
        P("dp", "tensor"),
        P("tensor"),
        P("tensor", "dp"),
        P(),
        P(),
        P(),
    )
    return jax.shard_map(shards, mesh=mesh, in_specs=in_specs, out_specs=out_specs, check_vma=False)
```

profile of v0, /device:TPU:0, one launch (start us, length us, event | category | flops | bytes accessed | tf_op | source)
XLA Modules:
  0.0 1302.5 jit_solution(1890085184275890445)
XLA Ops:
  8.0 3.1 fusion.59
  11.8 3.1 fusion.60
  15.7 3.1 convolution_convert_fusion.1
  18.8 1.5 reshape.145
  20.2 1.3 copy.72
  22.4 13.0 while.10
  37.6 4.7 fusion.73
  43.9 1.3 convert_element_type.128
  45.1 222.9 %all-reduce.6.cloned.1.call-done = f32[2048,768]{1,0:T(8,128)} async-done(((f32[2048,768]{1,0:T(8,128)}), f32[2048,768]{1,0:T(8,128)}) %all-reduce.6.cloned.1.call-update) | async-done | bytes 6291472 | tf_op jit(solution)/shard_map/psum | solution.py:154
  268.0 4.6 fusion.72
  275.3 18.3 %multiply_convert_fusion.1 = (bf16[2048,768]{1,0:T(8,128)(2,1)S(1)}, f32[2048,768]{1,0:T(8,128)}, f32[2048,768]{1,0:T(8,128)}) fusion(f32[768]{0:T(1024)S(1)} %copy-done.32, bf16[2048,768]{1,0:T(8,128)(2,1)S(1)} %fusion.58, bf16[768,768]{1,0:T(8,128)(2,1)S(1)} %copy-done), kind=kOutput, calls=%fused_computation.79 | convolution fusion | flops 2519728128 | bytes 20057088 | tf_op jit(solution)/shard_map/dot_general | solution.py:161
  293.6 1.7 copy-done.41
  295.4 4.5 fusion.74
  300.4 1.3 convert_element_type.130
  304.2 217.6 %all-reduce.8.cloned.1.call-done = f32[2048,768]{1,0:T(8,128)} async-done(((f32[2048,768]{1,0:T(8,128)}), f32[2048,768]{1,0:T(8,128)}) %all-reduce.8.cloned.1.call-update) | async-done | bytes 6291472 | tf_op jit(solution)/shard_map/psum | solution.py:167
  521.8 5.7 fusion.70
  529.4 3.6 fusion.52
  533.0 4.5 convert_reduce_fusion.1
  537.5 9.5 convert_reduce_fusion.2
  547.1 1.7 copy-done.40
  548.7 4.5 fusion.75
  553.5 221.7 %all-reduce.10.cloned.1.call-done = f32[2048,768]{1,0:T(8,128)} async-done(((f32[2048,768]{1,0:T(8,128)}), f32[2048,768]{1,0:T(8,128)}) %all-reduce.10.cloned.1.call-update) | async-done | bytes 6291472 | tf_op jit(solution)/shard_map/psum | solution.py:181
  775.2 8.7 multiply_reduce_fusion.2
  784.0 5.2 convert_reduce_fusion.3
  790.4 1.5 copy-done.3
  791.9 2.3 convolution_bitcast_fusion
  796.9 25.6 %while.27 = (s32[]{:T(128)}, bf16[4,512,192]{1,2,0:T(8,128)(2,1)S(1)}, bf16[4,512,192]{1,2,0:T(8,128)(2,1)}, bf16[4,512,192]{1,2,0:T(8,128)(2,1)}, bf16[4,512,3,...) while((s32[]{:T(128)}, ...), condition=%wide.region_17.18_spmd, body=%wide.region_15.17_spmd.sunk | while | flops 513243648 | bytes 26788472 | solution.py:195
  798.2 1.7 multiply_reduce_fusion.10
  804.6 1.7 multiply_reduce_fusion.10
  811.0 1.7 multiply_reduce_fusion.10
  817.5 1.7 multiply_reduce_fusion.10
  822.7 5.3 fusion.76
  831.5 3.9 add_add_fusion
  835.7 8.0 fusion.63
  843.8 7.0 fusion.78
  850.8 2.8 convolution_bitcast_fusion.3
  854.9 3.6 convolution_bitcast_fusion.2
  858.5 2.3 copy.90
  860.9 2.7 convolution_bitcast_fusion.1
  865.2 25.8 %all-reduce = (f32[192]{0:T(256)}, f32[192]{0:T(256)}, f32[768]{0:T(1024)}, f32[768]{0:T(1024)}, f32[768]{0:T(1024)}, /*index=5*/f32[768]{0:T(1024)}, f32[768]{0:T(1024)}, f32[768]{0:T(1024)}, f32[768]{0:T(1024)}) all-reduce(f32[192]{0:T(256)S(1)} %convert_reduce_fusion.5, ...), channel_id=1, replica_groups=mesh['dp'=8,'tensor'=4] {'dp'}, use_global_device_ids=true, to_apply=%region_21.22 | all-reduce | flops 5760 | bytes 46080 | tf_op jit(solution)/shard_map/psum | solution.py:214
  891.0 1.7 copy.95
  892.8 194.5 %all-reduce.12.cloned.1.call-done = f32[2048,768]{1,0:T(8,128)} async-done(((f32[2048,768]{1,0:T(8,128)}), f32[2048,768]{1,0:T(8,128)}) %all-reduce.12.cloned.1.call-update) | async-done | bytes 6291472 | tf_op jit(solution)/shard_map/psum | solution.py:213
  1087.3 8.1 add.177
  1095.4 37.2 %reduce-scatter.17.cloned.1.call-done = f32[768,96]{0,1:T(8,128)} async-done(((f32[768,768]{0,1:T(8,128)}), f32[768,96]{0,1:T(8,128)}) %reduce-scatter.17.cloned.1.call-update) | async-done | bytes 294928 | tf_op jit(solution)/shard_map/reduce_scatter | solution.py:234
  1132.5 46.8 %reduce-scatter.15.cloned.1.call-done = f32[96,768]{1,0:T(8,128)} async-done(((f32[768,768]{1,0:T(8,128)}), f32[96,768]{1,0:T(8,128)}) %reduce-scatter.15.cloned.1.call-update) | async-done | bytes 294928 | tf_op jit(solution)/shard_map/reduce_scatter | solution.py:233
  1179.3 38.7 %reduce-scatter.19.cloned.1.call-done = f32[96,192]{1,0:T(8,128)} async-done(((f32[768,192]{1,0:T(8,128)}), f32[96,192]{1,0:T(8,128)}) %reduce-scatter.19.cloned.1.call-update) | async-done | bytes 73744
  1218.1 38.8 %reduce-scatter.21.cloned.1.call-done = f32[96,192]{1,0:T(8,128)} async-done(((f32[768,192]{1,0:T(8,128)}), f32[96,192]{1,0:T(8,128)}) %reduce-scatter.21.cloned.1.call-update) | async-done | bytes 73744
  1256.8 38.6 %reduce-scatter.23.cloned.1.call-done = f32[96,192]{1,0:T(8,128)} async-done(((f32[768,192]{1,0:T(8,128)}), f32[96,192]{1,0:T(8,128)}) %reduce-scatter.23.cloned.1.call-update) | async-done | bytes 73744
  (202 shorter events, 56.9 us)
Async XLA Ops:
  7.2 268.1 %copy-start = (bf16[768,768]{1,0:T(8,128)(2,1)S(1)}, bf16[768,768]{1,0:T(8,128)(2,1)}, u32[]{:S(2)}) copy-start(bf16[768,768]{1,0:T(8,128)(2,1)} %param.31) | copy-start | bytes 3538948
  7.2 4.6 copy-start.39
  7.2 260.8 %all-reduce.6.cloned.1.call-start = ((), (), s32[]{:S(2)}) async-start(), calls=%async_computation.6 | async-start | bytes 12582912 | tf_op jit(solution)/shard_map/psum | solution.py:154
  37.5 5.1 copy-start.34
  37.5 5.1 copy-start.35
  37.5 5.7 copy-start.36
  42.3 479.5 %all-reduce.8.cloned.1.call-start = ((), (), s32[]{:S(2)}) async-start(), calls=%async_computation.7 | async-start | bytes 12582912 | tf_op jit(solution)/shard_map/psum | solution.py:167
  272.6 2.7 copy-start.2
  275.3 18.3 %copy-start.16 = (bf16[2048,768]{1,0:T(8,128)(2,1)}, bf16[2048,768]{1,0:T(8,128)(2,1)S(1)}, u32[]{:S(2)}) copy-start(bf16[2048,768]{1,0:T(8,128)(2,1)S(1)} %fusion.58) | copy-start | bytes 9437188
  275.3 20.1 %copy-start.37 = (bf16[768,768]{1,0:T(8,128)(2,1)S(1)}, bf16[768,768]{1,0:T(8,128)(2,1)}, u32[]{:S(2)}) copy-start(bf16[768,768]{1,0:T(8,128)(2,1)} %param.33) | copy-start | bytes 3538948
  299.8 475.4 %all-reduce.10.cloned.1.call-start = ((), (), s32[]{:S(2)}) async-start(), calls=%async_computation.8 | async-start | bytes 12582912 | tf_op jit(solution)/shard_map/psum | solution.py:181
  527.5 1.9 copy-start.5
  527.5 1.9 copy-start.22
  528.4 4.6 copy-start.30
  529.4 8.1 slice-start.2
  533.0 4.5 copy-start.33
  533.0 4.5 copy-start.38
  533.0 4.5 slice-start.3
  537.5 9.5 copy-start.4
  553.3 222.0 %copy-start.21 = (f32[768]{0:T(1024)S(1)}, f32[768]{0:T(1024)}, u32[]{:S(2)}) copy-start(f32[768]{0:T(1024)} %convert_element_type.125) | copy-start | bytes 9220
  553.3 337.7 %reduce-scatter.25.cloned.1.call-start = ((), (), s32[]{:S(2)}) async-start(), calls=%async_computation.15 | async-start | bytes 884736
  784.0 5.2 copy-start.17
  789.2 2.7 copy-start.3
  822.5 5.5 copy-start.10
  822.5 5.4 copy-start.15
  822.6 5.3 copy-start.6
  822.7 5.5 copy-start.18
  828.1 2.3 slice-start
  828.1 259.2 %all-reduce.12.cloned.1.call-start = ((), (), s32[]{:S(2)}) async-start(), calls=%async_computation.9 | async-start | bytes 12582912 | tf_op jit(solution)/shard_map/psum | solution.py:213
  828.2 2.2 copy-start.19
  828.2 3.3 slice-start.1
  835.4 297.1 %reduce-scatter.17.cloned.1.call-start = ((), (), s32[]{:S(2)}) async-start(), calls=%async_computation.11 | async-start | bytes 2654208 | tf_op jit(solution)/shard_map/reduce_scatter | solution.py:234
  843.7 7.1 copy-start.7
  843.7 335.6 %reduce-scatter.15.cloned.1.call-start = ((), (), s32[]{:S(2)}) async-start(), calls=%async_computation.10 | async-start | bytes 2654208 | tf_op jit(solution)/shard_map/reduce_scatter | solution.py:233
  850.8 10.1 copy-start.9
  850.8 367.3 %reduce-scatter.19.cloned.1.call-start = ((), (), s32[]{:S(2)}) async-start(), calls=%async_computation.12 | async-start | bytes 884736
  854.8 10.0 copy-start.13
  854.8 10.2 copy-start.11
  854.8 402.0 %reduce-scatter.21.cloned.1.call-start = ((), (), s32[]{:S(2)}) async-start(), calls=%async_computation.13 | async-start | bytes 884736
  858.5 6.7 copy-start.24
  858.5 6.7 copy-start.25
  858.5 6.7 copy-start.26
  858.5 6.7 copy-start.27
  858.5 6.7 copy-start.28
  858.5 6.7 copy-start.29
  858.5 6.7 copy-start.31
  860.8 434.6 %reduce-scatter.23.cloned.1.call-start = ((), (), s32[]{:S(2)}) async-start(), calls=%async_computation.14 | async-start | bytes 884736
  891.0 404.4 %copy-start.1 = (bf16[768,768]{1,0:T(8,128)(2,1)S(1)}, bf16[768,768]{1,0:T(8,128)(2,1)}, u32[]{:S(2)}) copy-start(bf16[768,768]{1,0:T(8,128)(2,1)} %param.31) | copy-start | bytes 3538948
  (8 other events, 10.1 us)
Sparse Core Ops, SparseCore 0:
  42.4 225.5 all-reduce.5
  300.0 221.7 all-reduce.7
  553.4 221.7 all-reduce.9
  828.2 33.9 reduce-scatter.24
  864.4 222.8 all-reduce.11
  1091.0 41.4 reduce-scatter.16
  1136.8 42.4 reduce-scatter.14
  1183.1 34.9 reduce-scatter.18
  1221.8 34.9 reduce-scatter.20
  1260.4 34.9 reduce-scatter.22
where the time goes:
time: 1310 us; the launch traced here: 1300 us
  waiting for transfers between devices  1060 us (81%)
  matrix products  110 us (8%)
  other arithmetic  58.7 us (4%)
  local copies, waits for them, and re-layouts  34.2 us (3%)
  blocking collectives  25.8 us (2%)
  between operations  15.1 us (1%)
    psum x1, waiting for transfers between devices, shards(): attn_total = lax.psum(attn_part, 'tensor') + b_output.astype(jnp.float32)  223 us
    psum x1, waiting for transfers between devices, shards(): lax.psum(times_transpose(grad_inner, w_inner), 'tensor')  222 us
    psum x1, waiting for transfers between devices, shards(): outer_total = lax.psum(outer_part, 'tensor') + b_outer.astype(jnp.float32)  218 us
    psum x1, waiting for transfers between devices, shards(): grad_inputs = grad_resid1 + lax.psum(input_part, 'tensor')  194 us
    unnamed x14, waiting for transfers between devices  116 us
    reduce_scatter x1, waiting for transfers between devices, shards(): lax.psum_scatter(grad_w_inner, 'dp', scatter_dimension=0, tiled=True)  46.8 us
    reduce_scatter x1, waiting for transfers between devices, shards(): lax.psum_scatter(grad_w_outer, 'dp', scatter_dimension=1, tiled=True)  37.2 us
  transfers between devices with their start and end apart: 10, of which 9 were waited for; matrix products, arithmetic and copies ran while one was open for 4% of the time, Pallas kernels for 0%

commit v1 on v0

--- a/solution.py
+++ b/solution.py
@@ -178,7 +178,9 @@
     grad_inner = gelu_pull(grad_active)[0].astype(jnp.bfloat16)
     grad_b_inner = column_sums(grad_inner)
     grad_w_inner = contract_rows(hidden_bf, grad_inner)
-    grad_hidden = grad_resid2 + lax.psum(times_transpose(grad_inner, w_inner), "tensor")
+    grad_hidden = grad_resid2 + jnp.sum(
+        lax.all_gather(times_transpose(grad_inner, w_inner), "tensor"), axis=0
+    )
     grad_resid1, grad_gain_attn, grad_shift_attn = norm_backward(
         grad_hidden, gain_one, normed_attn, inverse_attn
     )

time: 1310 us -> 1500 us (1.15)
  waiting for transfers between devices: 1060 us -> 1230 us
    all_gather x0 -> x1, waiting for transfers between devices: none -> 424 us  [shards(): lax.all_gather(times_transpose(grad_inner, w_inner), 'tensor')]
    psum x1 -> x0, waiting for transfers between devices: 222 us -> none  [shards(): lax.psum(times_transpose(grad_inner, w_inner), 'tensor')]
    psum x1, waiting for transfers between devices: 194 us -> 162 us  [shards(): grad_inputs = grad_resid1 + lax.psum(input_part, 'tensor')]
  transfers between devices with their start and end apart: 10 -> 10, of which waited for: 9 -> 9; matrix products, arithmetic and copies ran while one was open for 4% -> 6% of each run, Pallas kernels for 0% -> 0%
where the time goes in v1:
time: 1500 us; the launch traced here: 1490 us
  waiting for transfers between devices  1230 us (82%)
  matrix products  109 us (7%)
  other arithmetic  70.2 us (5%)
  local copies, waits for them, and re-layouts  42.3 us (3%)
  blocking collectives  26.5 us (2%)
    all_gather x1, waiting for transfers between devices, shards(): lax.all_gather(times_transpose(grad_inner, w_inner), 'tensor')  424 us
    psum x1, waiting for transfers between devices, shards(): attn_total = lax.psum(attn_part, 'tensor') + b_output.astype(jnp.float32)  224 us
    psum x1, waiting for transfers between devices, shards(): outer_total = lax.psum(outer_part, 'tensor') + b_outer.astype(jnp.float32)  218 us
    psum x1, waiting for transfers between devices, shards(): grad_inputs = grad_resid1 + lax.psum(input_part, 'tensor')  162 us
    unnamed x14, waiting for transfers between devices  116 us
    reduce_scatter x1, waiting for transfers between devices, shards(): lax.psum_scatter(grad_w_outer, 'dp', scatter_dimension=1, tiled=True)  46.8 us
    reduce_scatter x1, waiting for transfers between devices, shards(): lax.psum_scatter(grad_w_inner, 'dp', scatter_dimension=0, tiled=True)  37.2 us
  transfers between devices with their start and end apart: 10, of which 9 were waited for; matrix products, arithmetic and copies ran while one was open for 6% of the time, Pallas kernels for 0%

profile of v1, /device:TPU:0, one launch (start us, length us, event | category | flops | bytes accessed | tf_op | source)
XLA Modules:
  0.0 1491.9 jit_solution(14284575868259604310)
XLA Ops:
  8.7 3.1 fusion.59
  12.5 3.1 fusion.60
  16.3 3.1 convolution_convert_fusion.1
  19.4 1.5 reshape.145
  23.1 13.0 while.10
  38.2 4.7 fusion.73
  45.1 223.6 %all-reduce.5.cloned.1.call-done = f32[2048,768]{1,0:T(8,128)} async-done(((f32[2048,768]{1,0:T(8,128)}), f32[2048,768]{1,0:T(8,128)}) %all-reduce.5.cloned.1.call-update) | async-done | bytes 6291472 | tf_op jit(solution)/shard_map/psum | solution.py:154
  268.7 4.6 fusion.72
  276.0 18.3 %multiply_convert_fusion.1 = (bf16[2048,768]{1,0:T(8,128)(2,1)S(1)}, f32[2048,768]{1,0:T(8,128)}, f32[2048,768]{1,0:T(8,128)}) fusion(f32[768]{0:T(1024)S(1)} %copy-done.23, bf16[2048,768]{1,0:T(8,128)(2,1)S(1)} %fusion.58, bf16[768,768]{1,0:T(8,128)(2,1)S(1)} %copy-done), kind=kOutput, calls=%fused_computation.79 | convolution fusion | flops 2519728128 | bytes 20057088 | tf_op jit(solution)/shard_map/dot_general | solution.py:161
  294.3 1.6 copy-done.32
  295.9 4.5 fusion.74
  304.6 217.8 %all-reduce.7.cloned.1.call-done = f32[2048,768]{1,0:T(8,128)} async-done(((f32[2048,768]{1,0:T(8,128)}), f32[2048,768]{1,0:T(8,128)}) %all-reduce.7.cloned.1.call-update) | async-done | bytes 6291472 | tf_op jit(solution)/shard_map/psum | solution.py:167
  522.4 5.7 fusion.70
  530.0 3.6 fusion.52
  533.6 4.5 convert_reduce_fusion.1
  538.1 9.5 convert_reduce_fusion.2
  547.7 1.7 copy-done.31
  549.4 4.5 fusion.75
  554.6 423.6 %all-gather.3.cloned.1.call-done = f32[8192,768]{1,0:T(8,128)} async-done(((f32[2048,768]{1,0:T(8,128)}), f32[8192,768]{1,0:T(8,128)}) %all-gather.3.cloned.1.call-update) | async-done | bytes 25165840 | tf_op jit(solution)/shard_map/all_gather | solution.py:182
  978.2 12.7 reduce_sum.188
  990.9 8.1 multiply_reduce_fusion.2
  999.1 4.6 convert_reduce_fusion.3
  1003.7 2.7 copy-done.3
  1006.4 2.3 convolution_bitcast_fusion
  1008.7 4.0 convolution_convert_fusion
  1012.9 1.5 reshape.147
  1018.6 28.4 %while.27 = (s32[]{:T(128)}, bf16[4,512,192]{1,2,0:T(8,128)(2,1)}, bf16[4,512,192]{1,2,0:T(8,128)(2,1)}, bf16[4,512,192]{1,2,0:T(8,128)(2,1)}, bf16[4,512,3,64]{...) while((s32[]{:T(128)}, bf16[4,512,192]{1,2,0:T(8,128)(2,1)}, ...), condition=%wide.region_17.18_spmd, body=%wide.region_15.17_spmd.sunk | while | flops 513243648 | bytes 26787972 | solution.py:197
  1020.6 1.7 multiply_reduce_fusion.10
  1027.7 1.7 multiply_reduce_fusion.10
  1034.8 1.7 multiply_reduce_fusion.10
  1041.9 1.7 multiply_reduce_fusion.10
  1051.7 3.8 add_add_fusion
  1055.6 6.9 fusion.78
  1062.8 7.8 fusion.63
  1070.6 3.5 convolution_bitcast_fusion.2
  1074.1 2.3 copy.90
  1076.5 3.5 convolution_bitcast_fusion.3
  1080.0 2.3 copy.88
  1082.4 2.7 convolution_bitcast_fusion.1
  1086.6 26.5 %all-reduce = (f32[192]{0:T(256)}, f32[192]{0:T(256)}, f32[768]{0:T(1024)}, f32[768]{0:T(1024)}, f32[768]{0:T(1024)}, /*index=5*/f32[768]{0:T(1024)}, f32[768]{0:T(1024)}, f32[768]{0:T(1024)}, f32[768]{0:T(1024)}) all-reduce(f32[192]{0:T(256)S(1)} %convert_reduce_fusion.5, ...), channel_id=1, replica_groups=mesh['dp'=8,'tensor'=4] {'dp'}, use_global_device_ids=true, to_apply=%region_21.22 | all-reduce | flops 5760 | bytes 46080 | tf_op jit(solution)/shard_map/psum | solution.py:216
  1113.1 1.7 copy.95
  1114.8 161.9 %all-reduce.9.cloned.1.call-done = f32[2048,768]{1,0:T(8,128)} async-done(((f32[2048,768]{1,0:T(8,128)}), f32[2048,768]{1,0:T(8,128)}) %all-reduce.9.cloned.1.call-update) | async-done | bytes 6291472 | tf_op jit(solution)/shard_map/psum | solution.py:215
  1276.7 8.1 add.175
  1284.8 37.2 %reduce-scatter.15.cloned.1.call-done = f32[96,768]{1,0:T(8,128)} async-done(((f32[768,768]{1,0:T(8,128)}), f32[96,768]{1,0:T(8,128)}) %reduce-scatter.15.cloned.1.call-update) | async-done | bytes 294928 | tf_op jit(solution)/shard_map/reduce_scatter | solution.py:235
  1322.0 46.8 %reduce-scatter.17.cloned.1.call-done = f32[768,96]{0,1:T(8,128)} async-done(((f32[768,768]{0,1:T(8,128)}), f32[768,96]{0,1:T(8,128)}) %reduce-scatter.17.cloned.1.call-update) | async-done | bytes 294928 | tf_op jit(solution)/shard_map/reduce_scatter | solution.py:236
  1368.8 38.7 %reduce-scatter.21.cloned.1.call-done = f32[96,192]{1,0:T(8,128)} async-done(((f32[768,192]{1,0:T(8,128)}), f32[96,192]{1,0:T(8,128)}) %reduce-scatter.21.cloned.1.call-update) | async-done | bytes 73744
  1407.5 38.8 %reduce-scatter.19.cloned.1.call-done = f32[96,192]{1,0:T(8,128)} async-done(((f32[768,192]{1,0:T(8,128)}), f32[96,192]{1,0:T(8,128)}) %reduce-scatter.19.cloned.1.call-update) | async-done | bytes 73744
  1446.3 38.6 %reduce-scatter.23.cloned.1.call-done = f32[96,192]{1,0:T(8,128)} async-done(((f32[768,192]{1,0:T(8,128)}), f32[96,192]{1,0:T(8,128)}) %reduce-scatter.23.cloned.1.call-update) | async-done | bytes 73744
  (180 shorter events, 64.2 us)
Async XLA Ops:
  7.2 268.8 %copy-start = (bf16[768,768]{1,0:T(8,128)(2,1)S(1)}, bf16[768,768]{1,0:T(8,128)(2,1)}, u32[]{:S(2)}) copy-start(bf16[768,768]{1,0:T(8,128)(2,1)} %param.31) | copy-start | bytes 3538948
  7.2 261.5 %all-reduce.5.cloned.1.call-start = ((), (), s32[]{:S(2)}) async-start(), calls=%async_computation.6 | async-start | bytes 12582912 | tf_op jit(solution)/shard_map/psum | solution.py:154
  36.0 0.9 copy-start.8
  38.2 5.1 copy-start.25
  38.2 5.7 copy-start.26
  38.2 6.3 copy-start.27
  38.2 6.9 copy-start.28
  43.0 479.4 %all-reduce.7.cloned.1.call-start = ((), (), s32[]{:S(2)}) async-start(), calls=%async_computation.7 | async-start | bytes 12582912 | tf_op jit(solution)/shard_map/psum | solution.py:167
  273.3 2.7 copy-start.2
  273.3 0.9 copy-start.14
  273.3 0.9 copy-start.17
  274.2 1.8 copy-start.23
  276.0 18.3 %copy-start.9 = (bf16[2048,768]{1,0:T(8,128)(2,1)}, bf16[2048,768]{1,0:T(8,128)(2,1)S(1)}, u32[]{:S(2)}) copy-start(bf16[2048,768]{1,0:T(8,128)(2,1)S(1)} %fusion.58) | copy-start | bytes 9437188
  276.0 20.0 %copy-start.29 = (bf16[768,768]{1,0:T(8,128)(2,1)S(1)}, bf16[768,768]{1,0:T(8,128)(2,1)}, u32[]{:S(2)}) copy-start(bf16[768,768]{1,0:T(8,128)(2,1)} %param.33) | copy-start | bytes 3538948
  294.3 1.6 copy-start.32
  300.4 677.8 %all-gather.3.cloned.1.call-start = ((), (), s32[]{:S(2)}) async-start(), calls=%async_computation.11 | async-start | bytes 31457280 | tf_op jit(solution)/shard_map/all_gather | solution.py:182
  528.1 1.9 copy-start.5
  528.1 1.9 copy-start.16
  529.0 4.6 copy-start.21
  530.0 8.1 slice-start
  533.6 4.5 copy-start.24
  533.6 4.5 copy-start.30
  533.6 4.5 slice-start.1
  538.1 9.5 copy-start.4
  547.7 1.7 copy-start.31
  554.0 559.2 %reduce-scatter.25.cloned.1.call-start = ((), (), s32[]{:S(2)}) async-start(), calls=%async_computation.15 | async-start | bytes 884736
  978.2 12.7 copy-start.15
  1003.7 2.7 copy-start.3
  1003.7 5.0 copy-start.10
  1012.7 264.0 %all-reduce.9.cloned.1.call-start = ((), (), s32[]{:S(2)}) async-start(), calls=%async_computation.8 | async-start | bytes 12582912 | tf_op jit(solution)/shard_map/psum | solution.py:215
  1018.6 30.9 %copy-start.11 = (bf16[768,192]{0,1:T(8,128)(2,1)S(1)}, bf16[768,192]{0,1:T(8,128)(2,1)}, u32[]{:S(2)}) copy-start(bf16[768,192]{0,1:T(8,128)(2,1)} %param.22) | copy-start | bytes 884740
  1048.2 2.4 copy-start.12
  1050.5 1.1 copy-start.6
  1050.5 1.2 copy-start.13
  1055.5 266.4 %reduce-scatter.15.cloned.1.call-start = ((), (), s32[]{:S(2)}) async-start(), calls=%async_computation.9 | async-start | bytes 2654208 | tf_op jit(solution)/shard_map/reduce_scatter | solution.py:235
  1062.5 306.3 %reduce-scatter.17.cloned.1.call-start = ((), (), s32[]{:S(2)}) async-start(), calls=%async_computation.10 | async-start | bytes 2654208 | tf_op jit(solution)/shard_map/reduce_scatter | solution.py:236
  1070.6 336.9 %reduce-scatter.21.cloned.1.call-start = ((), (), s32[]{:S(2)}) async-start(), calls=%async_computation.13 | async-start | bytes 884736
  1076.4 10.0 copy-start.7
  1076.4 369.9 %reduce-scatter.19.cloned.1.call-start = ((), (), s32[]{:S(2)}) async-start(), calls=%async_computation.12 | async-start | bytes 884736
  1080.0 6.6 copy-start.18
  1080.0 6.6 copy-start.19
  1080.0 6.6 copy-start.20
  1080.0 6.6 copy-start.22
  1082.3 402.5 %reduce-scatter.23.cloned.1.call-start = ((), (), s32[]{:S(2)}) async-start(), calls=%async_computation.14 | async-start | bytes 884736
  1113.1 371.7 %copy-start.1 = (bf16[768,768]{1,0:T(8,128)(2,1)S(1)}, bf16[768,768]{1,0:T(8,128)(2,1)}, u32[]{:S(2)}) copy-start(bf16[768,768]{1,0:T(8,128)(2,1)} %param.31) | copy-start | bytes 3538948
Sparse Core Ops, SparseCore 0:
  43.1 225.5 all-reduce.4
  300.6 221.7 all-reduce.6
  554.1 424.1 all-gather.2
  1012.8 33.2 reduce-scatter.24
  1055.7 220.9 all-reduce.8
  1280.5 41.4 reduce-scatter.14
  1326.3 42.4 reduce-scatter.16
  1372.5 34.9 reduce-scatter.20
  1411.2 34.9 reduce-scatter.18
  1449.8 34.9 reduce-scatter.22
